TPU v7x, 32 devices: a whole 2x2x4 slice. The times are simulated.
32 devices in a mesh: sector: 4 (over x, core), op: 8 (over z, y).
Axes of the slice: x: 2, y: 2, z: 4, core: 2. Of those that a mesh axis runs over, the one named last changes fastest.
Arguments:
- wavefunction: bfloat16 [8, 512, 512], P('sector', 'op'), may hold values from -6 to 6
- sector_bases: bfloat16 [8, 512, 512], P('sector', 'op'), may hold values from -1 to 1
- left_env: bfloat16 [192, 512, 512], P(('sector', 'op')), may hold values from -0.25 to 0.25
- right_env: bfloat16 [192, 512, 512], P(('sector', 'op')), may hold values from -0.0546875 to 0.0546875
- pair_source: int32 [192], P(('sector', 'op')), may hold values from 0 to 7, as said below
- pair_target: int32 [192], P(('sector', 'op')), may hold values from 0 to 7
- sector_slot: int32 [8], replicated, may hold values from 0 to 7, as said below
- orders: int32 [8], replicated, may hold values from 256 to 512, as said below
Outputs:
- sigma_blocks: bfloat16 [8, 512, 512], P('sector', 'op')
- left_rotated: bfloat16 [192, 512, 512], P(('sector', 'op'))
Inputs may be any that keep to these rules, and one draw needn't show every extreme that they name: A permutation: sector s's blocks stand at slot sector_slot[s]. `pair_source`: the pairs held by index i of the sector axis have sources whose slots lie in i * 2 to (i + 1) * 2 - 1. `orders`: some sector has order exactly 512.
All inputs are finite; a program needn't handle non-finite values.
Results may differ from a plain program's by a relative error of at most 0.0049.
Values may be sent and summed in bfloat16 or wider, within the bound.
A program may use at most 128 MiB of HBM per device.

v0:
```python
import jax
import jax.numpy as jnp
from jax import lax
from jax.sharding import PartitionSpec as P


def slot_of(labels, sector_slot):
    sectors = sector_slot.shape[0]
    numbers = jnp.arange(sectors, dtype=jnp.int32)
    matches = labels[:, None] == numbers[None, :]
    return jnp.sum(jnp.where(matches, sector_slot[None, :], 0), axis=1)


def fold_rows(pick_source, stacked, left_env):
    chosen = jnp.einsum(
        "pq,qnk->pnk", pick_source, stacked, preferred_element_type=jnp.float32
    ).astype(jnp.bfloat16)
    return jnp.einsum("pin,pnk->pik", left_env, chosen, preferred_element_type=jnp.float32)


def per_device(
    wavefunction, sector_bases, left_env, right_env, pair_source, pair_target, sector_slot, orders
):
    sectors = sector_slot.shape[0]
    per_owner = wavefunction.shape[0]
    slab = wavefunction.shape[1]
    width = wavefunction.shape[2]
    owner_index = lax.axis_index("sector")
    row_begin = lax.axis_index("op") * slab
    numbers = jnp.arange(sectors, dtype=jnp.int32)
    placed = sector_slot[None, :] == numbers[:, None]
    slot_order = jnp.sum(jnp.where(placed, orders[None, :], 0), axis=1)
    local_order = lax.dynamic_slice_in_dim(slot_order, owner_index * per_owner, per_owner)
    columns = jnp.arange(width, dtype=jnp.int32)
    row_ids = row_begin + jnp.arange(slab, dtype=jnp.int32)
    inside = (row_ids[None, :, None] < local_order[:, None, None]) & (
        columns[None, None, :] < local_order[:, None, None]
    )
    masked = jnp.where(inside, wavefunction, jnp.zeros((), wavefunction.dtype))
    source_slot = slot_of(pair_source, sector_slot)
    target_slot = slot_of(pair_target, sector_slot)
    owner_slots = jnp.arange(per_owner, dtype=jnp.int32)
    pick_source = (source_slot[:, None] - owner_index * per_owner == owner_slots[None, :]).astype(
        jnp.bfloat16
    )
    pick_target = (target_slot[:, None] == numbers[None, :]).astype(jnp.bfloat16)
    pick_weight = pick_target.astype(jnp.float32)
    projected = fold_rows(
        pick_source, lax.all_gather(masked, "op", axis=1, tiled=True), left_env
    ).astype(jnp.bfloat16)
    owned_bases = lax.all_gather(sector_bases, "op", axis=1, tiled=True)
    chosen_source = jnp.einsum(
        "pq,qkj->pkj", pick_source, owned_bases, preferred_element_type=jnp.float32
    ).astype(jnp.bfloat16)
    half_rotated = jnp.einsum(
        "pik,pkj->pij", left_env, chosen_source, preferred_element_type=jnp.float32
    ).astype(jnp.bfloat16)
    chosen_target = jnp.einsum(
        "ps,skj->pkj",
        pick_target,
        lax.all_gather(owned_bases, "sector", axis=0, tiled=True),
        preferred_element_type=jnp.float32,
    ).astype(jnp.bfloat16)
    left_rotated = jnp.einsum(
        "pra,prc->pac", chosen_target, half_rotated, preferred_element_type=jnp.float32
    ).astype(jnp.bfloat16)
    products = jnp.einsum("pik,pjk->pij", projected, right_env, preferred_element_type=jnp.float32)
    partial_value = jnp.einsum(
        "ps,pij->sij", pick_weight, products, precision=lax.Precision.HIGHEST
    )
    owner_share = lax.psum_scatter(partial_value, "sector", scatter_dimension=0, tiled=True)
    sigma_part = lax.psum_scatter(owner_share, "op", scatter_dimension=1, tiled=True)
    sigma_blocks = jnp.where(inside, sigma_part, jnp.zeros((), jnp.float32)).astype(jnp.bfloat16)
    return (sigma_blocks, left_rotated)


def solution(mesh):
    placed = (
        P("sector", "op", None),
        P("sector", "op", None),
        P(("sector", "op"), None, None),
        P(("sector", "op"), None, None),
        P(("sector", "op")),
        P(("sector", "op")),
        P(),
        P(),
    )
    return jax.shard_map(
        per_device,
        mesh=mesh,
        in_specs=placed,
        out_specs=(P("sector", "op", None), P(("sector", "op"), None, None)),
        check_vma=False,
    )
```

profile of v0, /device:TPU:0, one launch (start us, length us, event | category | flops | bytes accessed | tf_op | source)
XLA Modules:
  0.0 310.0 jit_solution(12788211465308373763)
XLA Ops:
  7.2 0.0 copy-start
  7.2 0.0 all-gather.6.cloned.1.call-start
  7.2 1.8 copy.36
  9.1 0.0 all-gather.6.cloned.1.call-update
  9.1 0.0 all-gather.4.cloned.1.call-start
  9.2 0.8 select_reduce_fusion.2
  9.9 0.1 dynamic_slice.3
  10.0 0.1 iota_compare_fusion.3
  10.1 0.1 broadcast_compare_fusion
  10.2 1.8 and_select_fusion.1
  12.0 0.0 all-gather.4.cloned.1.call-update
  12.0 0.0 all-gather.8.cloned.1.call-start
  12.1 41.7 %all-gather.6.cloned.1.call-done = bf16[2,512,512]{2,0,1:T(2,128)(2,1)} async-done(((bf16[2,64,512]{2,0,1:T(2,128)(2,1)}), bf16[2,512,512]{2,0,1:T(2,128)(2,1)}) %all-gather.6.cloned.1.call-update) | async-done | bytes 1048592 | tf_op jit(solution)/shard_map/all_gather | solution.py:51
  53.7 2.4 copy.37
  56.1 0.0 all-gather.8.cloned.1.call-update
  56.1 0.0 reduce-scatter.2.cloned.1.call-start
  56.2 0.9 select_reduce_fusion.1
  57.1 38.4 %all-gather.4.cloned.1.call-done = bf16[2,512,512]{2,0,1:T(2,128)(2,1)} async-done(((bf16[2,64,512]{2,0,1:T(2,128)(2,1)}), bf16[2,512,512]{2,0,1:T(2,128)(2,1)}) %all-gather.4.cloned.1.call-update) | async-done | bytes 1048592 | tf_op jit(solution)/shard_map/all_gather | solution.py:49
  95.4 4.1 %convolution_convert_fusion.1 = bf16[6,512,512]{2,0,1:T(8,128)(2,1)} fusion(bf16[2,512,512]{2,0,1:T(2,128)(2,1)} %all-gather.4.cloned.1.call-done, s32[6]{0:T(128)S(1)} %broadcast_subtract_fusion), kind=kOutput, calls=%fused_computation.15 | convolution fusion | flops 7864332 | bytes 4194328 | tf_op jit(solution)/shard_map/pq,qnk->pnk/dot_general | solution.py:15
  99.6 0.0 copy-done
  99.6 10.8 %fusion.11 = f32[6,512,512]{2,1,0:T(8,128)} fusion(bf16[6,512,512]{2,1,0:T(8,128)(2,1)} %param.11, bf16[6,512,512]{2,1,0:T(8,128)(2,1)S(1)} %copy-done, bf16[6,512,512]{2,0,1:T(8,128)(2,1)} %convolution_convert_fusion.1), kind=kOutput, calls=%fused_computation.11 | convolution fusion | flops 3222798336 | bytes 15728640 | tf_op jit(solution)/shard_map/pik,pjk->pij/dot_general | solution.py:67
  110.4 15.1 %fusion = f32[8,512,512]{2,0,1:T(8,128)S(1)} fusion(f32[6,512,512]{2,1,0:T(8,128)} %fusion.11, s32[6]{0:T(128)S(1)} %get-tuple-element.10), kind=kOutput, calls=%fused_computation | convolution fusion | flops 150994992 | bytes 14680088 | tf_op jit(solution)/shard_map/ps,pij->sij/dot_general | solution.py:68
  125.5 8.1 %copy.34 = f32[8,512,512]{2,1,0:T(8,128)} copy(f32[8,512,512]{2,0,1:T(8,128)S(1)} %fusion) | data formatting | bytes 16777216 | tf_op jit(solution)/shard_map/ps,pij->sij/dot_general | solution.py:68
  133.6 0.0 copy-start.1
  133.6 0.0 reduce-scatter.2.cloned.1.call-update
  133.6 0.6 copy-done.1
  134.2 0.6 dynamic-slice
  135.4 4.1 %convolution_convert_fusion = bf16[6,512,512]{2,0,1:T(8,128)(2,1)} fusion(bf16[2,512,512]{2,0,1:T(2,128)(2,1)} %all-gather.6.cloned.1.call-done, s32[6]{0:T(128)S(1)} %broadcast_subtract_fusion), kind=kOutput, calls=%fused_computation.14 | convolution fusion | flops 7864332 | bytes 4194328 | tf_op jit(solution)/shard_map/pq,qkj->pkj/dot_general | solution.py:52
  139.6 0.0 all-gather.8.cloned.1.call-done
  139.6 7.7 %fusion.13 = bf16[6,512,512]{2,0,1:T(8,128)(2,1)} fusion(bf16[8,512,512]{2,1,0:T(8,128)(2,1)} %all-gather.8.cloned.1.call-done, s32[6]{0:T(128)S(1)} %get-tuple-element.10), kind=kOutput, calls=%fused_computation.13 | convolution fusion | flops 26738736 | bytes 7340056 | tf_op jit(solution)/shard_map/ps,skj->pkj/dot_general | solution.py:58
  147.3 11.2 %fusion.16 = bf16[6,512,512]{2,1,0:T(8,128)(2,1)} fusion(bf16[6,512,512]{2,0,1:T(8,128)(2,1)} %fusion.13, bf16[6,512,512]{2,1,0:T(8,128)(2,1)S(1)} %copy-done, bf16[6,512,512]{2,0,1:T(8,128)(2,1)} %convolution_convert_fusion), kind=kOutput, calls=%fused_computation.16 | convolution fusion | flops 3224371200 | bytes 12582912 | tf_op jit(solution)/shard_map/pra,prc->pac/dot_general | solution.py:64
  158.5 46.2 %reduce-scatter.2.cloned.1.call-done = f32[2,512,512]{2,1,0:T(8,128)} async-done(((f32[8,512,512]{2,1,0:T(8,128)}), f32[2,512,512]{2,1,0:T(8,128)}) %reduce-scatter.2.cloned.1.call-update) | async-done | bytes 2097168 | tf_op jit(solution)/shard_map/reduce_scatter | solution.py:71
  204.7 4.6 %copy.35 = f32[2,512,512]{2,0,1:T(2,128)} copy(f32[2,512,512]{2,1,0:T(8,128)} %reduce-scatter.2.cloned.1.call-done) | data formatting | bytes 4194304 | tf_op jit(solution)/shard_map/reduce_scatter | solution.py:71
  209.2 92.5 %all-reduce.2 = bf16[2,512,512]{2,0,1:T(2,128)(2,1)} all-reduce(f32[2,512,512]{2,0,1:T(2,128)} %copy.35), channel_id=3, replica_groups=mesh['sector'=4,'op'=8] {'op'}, use_global_device_ids=true, to_apply=%region_4.5.clone | all-reduce | flops 524288 | bytes 3145728
  301.7 1.1 fusion.29
  302.8 0.7 copy.41
  (2 shorter events, 0.0 us)
Async XLA Ops:
  7.2 92.4 %copy-start = (bf16[6,512,512]{2,1,0:T(8,128)(2,1)S(1)}, bf16[6,512,512]{2,1,0:T(8,128)(2,1)}, u32[]{:S(2)}) copy-start(bf16[6,512,512]{2,1,0:T(8,128)(2,1)} %param.10) | copy-start | bytes 9437188
  7.2 46.5 %all-gather.6.cloned.1.call-start = ((), (), s32[]{:S(2)}) async-start(), calls=%async_computation.3 | async-start | bytes 1179648 | tf_op jit(solution)/shard_map/all_gather | solution.py:51
  9.1 86.3 %all-gather.4.cloned.1.call-start = ((), (), s32[]{:S(2)}) async-start(), calls=%async_computation.1 | async-start | bytes 1179648 | tf_op jit(solution)/shard_map/all_gather | solution.py:49
  12.0 127.6 %all-gather.8.cloned.1.call-start = ((), (), s32[]{:S(2)}) async-start(), calls=%async_computation.4 | async-start | bytes 5242880 | tf_op jit(solution)/shard_map/all_gather | solution.py:61
  56.1 148.5 %reduce-scatter.2.cloned.1.call-start = ((), (), s32[]{:S(2)}) async-start(), calls=%async_computation.2 | async-start | bytes 10485760 | tf_op jit(solution)/shard_map/reduce_scatter | solution.py:71
  133.6 0.7 copy-start.1
Sparse Core Ops, SparseCore 0:
  10.7 42.9 all-gather.5
  56.4 38.9 all-gather.3
  97.6 33.1 all-gather.7
  133.7 70.9 reduce-scatter.1
where the time goes:
time: 310 us
  waiting for transfers between devices  126 us (41%)
  blocking collectives  92.5 us (30%)
  matrix products  53.1 us (17%)
  local copies, waits for them, and re-layouts  18.8 us (6%)
  between operations  14.5 us (5%)
  other arithmetic  4.79 us (2%)
    unnamed x1, blocking collectives  92.5 us
    reduce_scatter x1, waiting for transfers between devices, per_device(): lax.psum_scatter(partial_value, 'sector', scatter_dimension=0, tiled=True)  46.2 us
    all_gather x1, waiting for transfers between devices, per_device(): owned_bases = lax.all_gather(sector_bases, 'op', axis=1, tiled=True)  41.7 us
    all_gather x1, waiting for transfers between devices, per_device(): lax.all_gather(masked, 'op', axis=1, tiled=True)  38.4 us
    dot_general x1, matrix products, per_device(): jnp.einsum('ps,pij->sij', pick_weight, products, precision=lax.Precision....  15.1 us
    dot_general x1, matrix products, per_device(): jnp.einsum('pra,prc->pac', chosen_target, half_rotated, preferred_element...  11.2 us
    dot_general x1, matrix products, per_device(): jnp.einsum('pik,pjk->pij', projected, right_env, preferred_element_type=j...  10.8 us
    dot_general x1, local copies, waits for them, and re-layouts, per_device(): jnp.einsum('ps,pij->sij', pick_weight, products, precision=lax.Precision....  8.07 us
  transfers between devices with their start and end apart: 4, of which 3 were waited for; matrix products, arithmetic and copies ran while one was open for 22% of the time, Pallas kernels for 0%

commit v1 on v0

v1 whole, which is shorter than its diff:
```python
import functools

import jax
import jax.numpy as jnp
from jax import lax
from jax.experimental import pallas as pl
from jax.experimental.pallas import tpu as pltpu
from jax.sharding import PartitionSpec as P

MESH = pl.DeviceIdType.MESH
ANY = pl.BlockSpec(memory_space=pl.ANY)
VMEM = pl.BlockSpec(memory_space=pltpu.VMEM)
SMEM = pl.BlockSpec(memory_space=pltpu.SMEM)


def grid_of(n_sector, n_op):
    cores = 2 if n_sector % 2 == 0 else 1
    ny = 1
    while ny * ny * 4 <= n_op and n_op % (ny * 2) == 0:
        ny *= 2
    return n_sector // cores, cores, n_op // ny, ny


class Place:
    def __init__(self, dims):
        self.dims = dims
        nx, nc, nz, ny = dims
        sector, op = lax.axis_index("sector"), lax.axis_index("op")
        self.x, self.c = sector // nc, sector % nc
        self.z, self.y = op // ny, op % ny

    def at(self, x=0, c=0, z=0, y=0):
        nx, nc, nz, ny = self.dims
        return (
            lax.rem(self.x + x, nx),
            lax.rem(self.c + c, nc),
            lax.rem(self.z + z, nz),
            lax.rem(self.y + y, ny),
        )

    def device(self, **shift):
        nx, nc, nz, ny = self.dims
        x, c, z, y = self.at(**shift)
        return (x * nc + c, z * ny + y)

    def greet(self):
        barrier = pltpu.get_barrier_semaphore()
        count = 0
        for name, n in zip("xczy", self.dims):
            for shift in range(1, n):
                pl.semaphore_signal(
                    barrier, inc=1, device_id=self.device(**{name: shift}), device_id_type=MESH
                )
                count += 1
        pl.semaphore_wait(barrier, count)


def remote(src, dst, send, recv, device):
    return pltpu.make_async_remote_copy(
        src_ref=src, dst_ref=dst, send_sem=send, recv_sem=recv, device_id=device, device_id_type=MESH
    )


def gather_kernel(
    dims, wave_ref, base_ref, wave_all, base_all,
    local, wzs, wzr, wys, wyr, bzs, bzr, bys, byr, bxs, bxr, bcs, bcr,
):
    nx, nc, nz, ny = dims
    me = Place(dims)
    per_owner, slab, _ = wave_ref.shape

    def rows(z, y):
        return pl.ds((z * ny + y) * slab, slab)

    def wave(d, e):
        _, _, z, y = me.at(z=nz - d, y=ny - e)
        return wave_all.at[:, rows(z, y), :]

    def base(d, e, f, g):
        x, c, z, y = me.at(x=nx - f, c=nc - g, z=nz - d, y=ny - e)
        return base_all.at[pl.ds((x * nc + c) * per_owner, per_owner), rows(z, y), :]

    keep_wave = pltpu.make_async_copy(wave_ref, wave(0, 0), local.at[0])
    keep_base = pltpu.make_async_copy(base_ref, base(0, 0, 0, 0), local.at[1])

    def wave_z(d):
        return remote(wave_ref, wave(0, 0), wzs.at[d], wzr.at[d], me.device(z=d))

    def wave_y(d, e, src):
        return remote(src, wave(d, 0), wys.at[e, d], wyr.at[e, d], me.device(y=e))

    def base_z(d):
        return remote(base_ref, base(0, 0, 0, 0), bzs.at[d], bzr.at[d], me.device(z=d))

    def base_y(d, e, src):
        return remote(src, base(d, 0, 0, 0), bys.at[e, d], byr.at[e, d], me.device(y=e))

    def base_x(d, e, f, src):
        return remote(src, base(d, e, 0, 0), bxs.at[f, e, d], bxr.at[f, e, d], me.device(x=f))

    def base_c(d, e, f, g, src):
        return remote(src, base(d, e, f, 0), bcs.at[f, e, d], bcr.at[f, e, d], me.device(c=g))

    me.greet()
    keep_wave.start()
    keep_base.start()
    for e in range(1, ny):
        wave_y(0, e, wave_ref).start()
    for d in range(1, nz):
        wave_z(d).start()
    for f in range(1, nx):
        base_x(0, 0, f, base_ref).start()
    for g in range(1, nc):
        base_c(0, 0, 0, g, base_ref).start()
    for e in range(1, ny):
        base_y(0, e, base_ref).start()
    for d in range(1, nz):
        base_z(d).start()
    for d in range(1, nz):
        wave_z(d).wait_recv()
        for e in range(1, ny):
            wave_y(d, e, wave(d, 0)).start()

    def forward_x(d, e):
        for f in range(1, nx):
            base_x(d, e, f, base(d, e, 0, 0)).start()
        for g in range(1, nc):
            base_c(d, e, 0, g, base(d, e, 0, 0)).start()

    for e in range(1, ny):
        base_y(0, e, base(0, 0, 0, 0)).wait_recv()
        forward_x(0, e)
    for d in range(1, nz):
        base_z(d).wait_recv()
        for e in range(1, ny):
            base_y(d, e, base(d, 0, 0, 0)).start()
        forward_x(d, 0)
    for e in range(1, ny):

        @pl.loop(1, nz)
        def _(d):
            base_y(d, e, base(d, 0, 0, 0)).wait_recv()
            forward_x(d, e)

    for f in range(1, nx):
        for e in range(ny):

            @pl.loop(0, nz)
            def _(d):
                base_x(d, e, f, base(d, e, 0, 0)).wait_recv()
                for g in range(1, nc):
                    base_c(d, e, f, g, base(d, e, f, 0)).start()

    keep_wave.wait()
    keep_base.wait()
    for d in range(1, nz):
        wave_z(d).wait_send()
        base_z(d).wait_send()
    for e in range(1, ny):

        @pl.loop(0, nz)
        def _(d):
            wave_y(d, e, wave(d, 0)).wait()
            base_y(d, e, base(d, 0, 0, 0)).wait_send()

    for e in range(ny):

        @pl.loop(0, nz)
        def _(d):
            for f in range(1, nx):
                base_x(d, e, f, base(d, e, 0, 0)).wait_send()
            for f in range(nx):
                for g in range(1, nc):
                    base_c(d, e, f, g, base(d, e, f, 0)).wait()


def gather(dims, wavefunction, sector_bases):
    nx, nc, nz, ny = dims
    per_owner, slab, width = wavefunction.shape
    dma = pltpu.SemaphoreType.DMA
    return pl.pallas_call(
        functools.partial(gather_kernel, dims),
        out_shape=(
            jax.ShapeDtypeStruct((per_owner, nz * ny * slab, width), wavefunction.dtype),
            jax.ShapeDtypeStruct((nx * nc * per_owner, nz * ny * slab, width), sector_bases.dtype),
        ),
        in_specs=[VMEM, VMEM],
        out_specs=(ANY, ANY),
        scratch_shapes=[dma((2,))]
        + [dma((nz,)), dma((nz,)), dma((ny, nz)), dma((ny, nz))] * 2
        + [dma((nx, ny, nz))] * 4,
        compiler_params=pltpu.CompilerParams(collective_id=0, has_side_effects=True),
        name="gather",
    )(wavefunction, sector_bases)


def order_of(slot, sector_slot, orders, sectors):
    total = jnp.int32(0)
    for i in range(sectors):
        total = total + jnp.where(sector_slot[i] == slot, orders[i], 0)
    return total


def pair_kernel(
    sectors, source, target, sector_slot, orders, wave, bases, left, right, sigma, rotated, masked, total
):
    step = pl.program_id(0)
    per_owner, width, _ = wave.shape
    first = lax.axis_index("sector") * per_owner

    @pl.when(step == 0)
    def _():
        total[...] = jnp.zeros_like(total)
        row = lax.broadcasted_iota(jnp.int32, (width, width), 0)
        column = lax.broadcasted_iota(jnp.int32, (width, width), 1)
        for j in range(per_owner):
            order = order_of(first + j, sector_slot, orders, sectors)
            inside = jnp.maximum(row, column) < order
            masked[j] = jnp.where(inside, wave[j], jnp.zeros((), wave.dtype))

    a = sector_slot[source[step]]
    b = sector_slot[target[step]]
    block = left[0]
    projected = jnp.dot(block, masked[a - first], preferred_element_type=jnp.float32)
    half = jnp.dot(block, bases[a], preferred_element_type=jnp.float32)
    total[b] += lax.dot_general(
        projected.astype(block.dtype), right[0], (((1,), (1,)), ((), ())),
        preferred_element_type=jnp.float32,
    )
    rotated[0] = lax.dot_general(
        bases[b], half.astype(block.dtype), (((0,), (0,)), ((), ())),
        preferred_element_type=jnp.float32,
    ).astype(rotated.dtype)

    @pl.when(step == pl.num_programs(0) - 1)
    def _():
        @pl.loop(0, total.shape[0])
        def _(q):
            sigma[q] = total[q].astype(sigma.dtype)


def pairs(wave, bases, left, right, source, target, sector_slot, orders):
    count, width, _ = left.shape
    sectors = sector_slot.shape[0]
    whole = lambda shape: pl.BlockSpec(
        shape, lambda p, *_: (0, 0, 0), pipeline_mode=pl.Buffered(1)
    )
    each = pl.BlockSpec((1, width, width), lambda p, *_: (p, 0, 0))
    return pl.pallas_call(
        functools.partial(pair_kernel, sectors),
        out_shape=(
            jax.ShapeDtypeStruct(bases.shape, jnp.bfloat16),
            jax.ShapeDtypeStruct(left.shape, left.dtype),
        ),
        grid_spec=pltpu.PrefetchScalarGridSpec(
            num_scalar_prefetch=4,
            grid=(count,),
            in_specs=[whole(wave.shape), whole(bases.shape), each, each],
            out_specs=(whole(bases.shape), each),
            scratch_shapes=[
                pltpu.VMEM(wave.shape, wave.dtype),
                pltpu.VMEM(bases.shape, jnp.float32),
            ],
        ),
        compiler_params=pltpu.CompilerParams(
            dimension_semantics=("arbitrary",), vmem_limit_bytes=60 * 1024 * 1024
        ),
        name="pairs",
    )(source, target, sector_slot, orders, wave, bases, left, right)


def reduce_kernel(
    dims, sectors, part, sector_slot, orders, out,
    got_c, send_1, got_1, mid, send_2, got_2, held, send_3, got_3,
    cs, cr, s1, r1, s2, r2, s3, r3,
):
    nx, nc, nz, ny = dims
    me = Place(dims)
    per_owner, slab, width = out.shape
    strip = ny * slab
    f32, bf16 = jnp.float32, jnp.bfloat16
    first = "xy"
    size = {"x": nx, "y": ny}

    def axes(j):
        return ("x", "y") if j % 2 == 0 else ("y", "x")

    def zq(d):
        return lax.rem(me.z + d, nz)

    def core_copy(x, j, d):
        slot = (x * nc + lax.rem(me.c + 1, nc)) * per_owner + j
        return remote(
            part.at[slot, pl.ds(zq(d) * strip, strip), :], got_c.at[d, j, x],
            cs.at[d, j, x], cr.at[d, j, x], me.device(c=1),
        )

    def copy_1(j, d, k):
        return remote(
            send_1.at[d, j, k], got_1.at[d, j, k], s1.at[d, j, k], r1.at[d, j, k],
            me.device(**{axes(j)[0]: k}),
        )

    def copy_2(j, d, k):
        return remote(
            send_2.at[d, j, k], got_2.at[d, j, k], s2.at[d, j, k], r2.at[d, j, k],
            me.device(**{axes(j)[1]: k}),
        )

    def copy_3(j, d):
        return remote(
            send_3.at[d, j], got_3.at[d, j], s3.at[d, j], r3.at[d, j], me.device(z=d)
        )

    def unit(d):
        return lax.rem(d + 1, nz)

    me.greet()
    if nc > 1:

        @pl.loop(0, nz)
        def _(i):
            for j in range(per_owner):
                for x in range(nx):
                    core_copy(x, j, unit(i)).start()

    @pl.loop(0, nz)
    def _(i):
        d = unit(i)
        for j in range(per_owner):
            n1 = size[axes(j)[0]]
            n2 = size[axes(j)[1]]

            def summed(x, row, count):
                slot = (x * nc + me.c) * per_owner + j
                value = part[slot, pl.ds(zq(d) * strip + row, count), :].astype(f32)
                if nc > 1:
                    value = value + got_c[d, j, x, pl.ds(row, count), :].astype(f32)
                return value

            if nc > 1:
                for x in range(nx):
                    core_copy(x, j, d).wait_recv()
            for k in list(range(1, n1)) + [0]:
                for m in range(n2):
                    if axes(j)[0] == "x":
                        x, y = lax.rem(me.x + k, nx), m
                    else:
                        x, y = m, lax.rem(me.y + k, ny)
                    value = summed(x, pl.multiple_of(y * slab, slab), slab)
                    if k:
                        send_1[d, j, k, m] = value.astype(bf16)
                    else:
                        mid[d, j, m] = value
                if k:
                    copy_1(j, d, k).start()

    @pl.loop(0, nz)
    def _(i):
        d = unit(i)
        for j in range(per_owner):
            axis_1, axis_2 = axes(j)
            n1, n2 = size[axis_1], size[axis_2]
            for k in range(1, n1):
                copy_1(j, d, k).wait_recv()
            for h in list(range(1, n2)) + [0]:
                m = lax.rem(getattr(me, axis_2) + h, n2)
                value = mid[d, j, m]
                for k in range(1, n1):
                    value = value + got_1[d, j, k, m].astype(f32)
                if h:
                    send_2[d, j, h] = value.astype(bf16)
                    copy_2(j, d, h).start()
                else:
                    held[d, j] = value

    def stage_3(d, j):
        for h in range(1, size[axes(j)[1]]):
            copy_2(j, d, h).wait_recv()
        value = held[d, j]
        for h in range(1, size[axes(j)[1]]):
            value = value + got_2[d, j, h].astype(f32)
        return value

    @pl.loop(1, nz)
    def _(d):
        for j in range(per_owner):
            send_3[d, j] = stage_3(d, j).astype(bf16)
            copy_3(j, d).start()

    own = (me.x * nc + me.c) * per_owner
    row = lax.broadcasted_iota(jnp.int32, (slab, width), 0) + (me.z * ny + me.y) * slab
    column = lax.broadcasted_iota(jnp.int32, (slab, width), 1)
    for j in range(per_owner):
        value = stage_3(0, j)
        for d in range(1, nz):
            copy_3(j, d).wait_recv()
            value = value + got_3[d, j].astype(f32)
        order = order_of(own + j, sector_slot, orders, sectors)
        inside = jnp.maximum(row, column) < order
        out[j] = jnp.where(inside, value, 0.0).astype(out.dtype)

    @pl.loop(0, nz)
    def _(d):
        for j in range(per_owner):
            if nc > 1:
                for x in range(nx):
                    core_copy(x, j, d).wait_send()
            for k in range(1, size[axes(j)[0]]):
                copy_1(j, d, k).wait_send()
            for h in range(1, size[axes(j)[1]]):
                copy_2(j, d, h).wait_send()

    @pl.loop(1, nz)
    def _(d):
        for j in range(per_owner):
            copy_3(j, d).wait_send()


def reduce(dims, part, sector_slot, orders, slab):
    nx, nc, nz, ny = dims
    sectors, _, width = part.shape
    per_owner = sectors // (nx * nc)
    most = max(nx, ny)
    dma = pltpu.SemaphoreType.DMA
    bf16, f32 = jnp.bfloat16, jnp.float32
    return pl.pallas_call(
        functools.partial(reduce_kernel, dims, sectors),
        out_shape=jax.ShapeDtypeStruct((per_owner, slab, width), bf16),
        in_specs=[VMEM, SMEM, SMEM],
        out_specs=VMEM,
        scratch_shapes=[
            pltpu.VMEM((nz, per_owner, nx, ny * slab, width), bf16),
            pltpu.VMEM((nz, per_owner, most, most, slab, width), bf16),
            pltpu.VMEM((nz, per_owner, most, most, slab, width), bf16),
            pltpu.VMEM((nz, per_owner, most, slab, width), f32),
            pltpu.VMEM((nz, per_owner, most, slab, width), bf16),
            pltpu.VMEM((nz, per_owner, most, slab, width), bf16),
            pltpu.VMEM((nz, per_owner, slab, width), f32),
            pltpu.VMEM((nz, per_owner, slab, width), bf16),
            pltpu.VMEM((nz, per_owner, slab, width), bf16),
        ]
        + [dma((nz, per_owner, nx))] * 2
        + [dma((nz, per_owner, most))] * 4
        + [dma((nz, per_owner))] * 2,
        compiler_params=pltpu.CompilerParams(
            collective_id=1, has_side_effects=True, vmem_limit_bytes=60 * 1024 * 1024
        ),
        name="reduce",
    )(part, sector_slot, orders)


def solution(mesh):
    dims = grid_of(mesh.shape["sector"], mesh.shape["op"])

    def per_device(
        wavefunction, sector_bases, left_env, right_env, pair_source, pair_target, sector_slot, orders
    ):
        wave, bases = gather(dims, wavefunction, sector_bases)
        part, left_rotated = pairs(
            wave, bases, left_env, right_env, pair_source, pair_target, sector_slot, orders
        )
        sigma_blocks = reduce(dims, part, sector_slot, orders, wavefunction.shape[1])
        return sigma_blocks, left_rotated

    placed = (
        P("sector", "op", None),
        P("sector", "op", None),
        P(("sector", "op"), None, None),
        P(("sector", "op"), None, None),
        P(("sector", "op")),
        P(("sector", "op")),
        P(),
        P(),
    )
    return jax.shard_map(
        per_device,
        mesh=mesh,
        in_specs=placed,
        out_specs=(P("sector", "op", None), P(("sector", "op"), None, None)),
        check_vma=False,
    )
```

time: 310 us -> 99.2 us (0.32)
  waiting for transfers between devices: 126 us -> 0 us
  Pallas kernels: 0 us -> 96.3 us
  blocking collectives: 92.5 us -> 0 us
  matrix products: 53.1 us -> 0 us
  local copies, waits for them, and re-layouts: 18.8 us -> 1.57 us
  between operations: 14.5 us -> 0.65 us
  other arithmetic: 4.79 us -> 0 us
    pallas_call x0 -> x3, Pallas kernels: none -> 96.3 us  [the longest x1 45 us: gather(): pl.pallas_call(functools.partial(gather_kernel, dims), out_shape=(jax.Sha...]
    unnamed x1 -> x0, blocking collectives: 92.5 us -> none
    all_gather x3 -> x0, waiting for transfers between devices: 80 us -> none  [the longest x1 41.7 us: per_device(): owned_bases = lax.all_gather(sector_bases, 'op', axis=1, tiled=True)]
    dot_general x6 -> x0, matrix products: 53.1 us -> none  [the longest x1 15.1 us: per_device(): jnp.einsum('ps,pij->sij', pick_weight, products, precision=lax.Precision....]
    reduce_scatter x1 -> x0, waiting for transfers between devices: 46.2 us -> none  [per_device(): lax.psum_scatter(partial_value, 'sector', scatter_dimension=0, tiled=True)]
    dot_general x1 -> x0, local copies, waits for them, and re-layouts: 8.07 us -> none  [per_device(): jnp.einsum('ps,pij->sij', pick_weight, products, precision=lax.Precision....]
    reduce_scatter x1 -> x0, local copies, waits for them, and re-layouts: 4.55 us -> none  [per_device(): lax.psum_scatter(partial_value, 'sector', scatter_dimension=0, tiled=True)]
  transfers between devices with their start and end apart: 4 -> 0, of which waited for: 3 -> 0; matrix products, arithmetic and copies ran while one was open for 22% -> 0% of each run, Pallas kernels for 0% -> 0%
where the time goes in v1:
time: 99.2 us; the launch traced here: 98.5 us
  Pallas kernels  96.3 us (97%)
  local copies, waits for them, and re-layouts  1.57 us (2%)
    pallas_call x1, Pallas kernels, gather(): pl.pallas_call(functools.partial(gather_kernel, dims), out_shape=(jax.Sha...  45 us
    pallas_call x1, Pallas kernels, reduce(): pl.pallas_call(functools.partial(reduce_kernel, dims, sectors), out_shape...  36.6 us
    pallas_call x1, Pallas kernels, pairs(): pl.pallas_call(functools.partial(pair_kernel, sectors), out_shape=(jax.Sh...  14.8 us

profile of v1, /device:TPU:0, one launch (start us, length us, event | category | flops | bytes accessed | tf_op | source)
XLA Modules:
  0.0 98.5 jit_solution(5553990851997045561)
XLA Ops:
  0.6 45.0 %gather.1 = (bf16[2,512,512]{2,1,0:T(8,128)(2,1)}, bf16[8,512,512]{2,1,0:T(8,128)(2,1)}) custom-call(bf16[2,64,512]{2,1,0:T(8,128)(2,1)} %wave_ref.1, bf16[2,64,512]{2,1,0:T(8,128)(2,1)} %base_ref.1), custom_call_target="tpu_custom_call" | custom-call | tf_op jit(solution)/shard_map/gather/pallas_call | solution.py:181
  45.6 14.8 %pairs.1 = (bf16[8,512,512]{2,1,0:T(8,128)(2,1)}, bf16[6,512,512]{2,1,0:T(8,128)(2,1)}) custom-call(s32[6]{0:T(128)} %source.1, s32[6]{0:T(128)} %target.1, s32[8]{0:T(128)} %sector_slot.3, s32[8]{0:T(128)} %orders.3, bf16[2,512,512]{2,1,0:T(8,128)(2,1)} %get-tuple-element.6.wave, bf16[8,512,512]{2,1,0:T(8,128)(2,1)} %get-tuple-element.7.bases, ...), custom_call_target="tpu_custom_call" | custom-call | tf_op jit(solution)/shard_map/pairs/pallas_call | solution.py:249
  60.4 36.6 %reduce.1 = bf16[2,64,512]{2,1,0:T(8,128)(2,1)} custom-call(bf16[8,512,512]{2,1,0:T(8,128)(2,1)} %get-tuple-element.8.part, s32[8]{0:T(128)} %sector_slot.3, s32[8]{0:T(128)} %orders.3), custom_call_target="tpu_custom_call" | custom-call | tf_op jit(solution)/shard_map/reduce/pallas_call | solution.py:427
  97.0 1.6 %copy.11 = bf16[2,64,512]{2,1,0:T(8,128)(2,1)} copy(bf16[2,64,512]{2,1,0:T(8,128)(2,1)} %reduce.1) | data formatting | bytes 262144

commit v2 on v1

v2 whole, which is shorter than its diff:
```python
import functools

import jax
import jax.numpy as jnp
from jax import lax
from jax.experimental import pallas as pl
from jax.experimental.pallas import tpu as pltpu
from jax.sharding import PartitionSpec as P

MESH = pl.DeviceIdType.MESH
ANY = pl.BlockSpec(memory_space=pl.ANY)
VMEM = pl.BlockSpec(memory_space=pltpu.VMEM)
SMEM = pl.BlockSpec(memory_space=pltpu.SMEM)


def grid_of(n_sector, n_op):
    cores = 2 if n_sector % 2 == 0 else 1
    ny = 1
    while ny * ny * 4 <= n_op and n_op % (ny * 2) == 0:
        ny *= 2
    return n_sector // cores, cores, n_op // ny, ny


class Place:
    def __init__(self, dims):
        self.dims = dims
        nx, nc, nz, ny = dims
        sector, op = lax.axis_index("sector"), lax.axis_index("op")
        self.x, self.c = sector // nc, sector % nc
        self.z, self.y = op // ny, op % ny

    def at(self, x=0, c=0, z=0, y=0):
        nx, nc, nz, ny = self.dims
        return (
            lax.rem(self.x + x, nx),
            lax.rem(self.c + c, nc),
            lax.rem(self.z + z, nz),
            lax.rem(self.y + y, ny),
        )

    def device(self, **shift):
        nx, nc, nz, ny = self.dims
        x, c, z, y = self.at(**shift)
        return (x * nc + c, z * ny + y)

    def greet(self):
        barrier = pltpu.get_barrier_semaphore()
        count = 0
        for name, n in zip("xczy", self.dims):
            for shift in range(1, n):
                pl.semaphore_signal(
                    barrier, inc=1, device_id=self.device(**{name: shift}), device_id_type=MESH
                )
                count += 1
        pl.semaphore_wait(barrier, count)


def remote(src, dst, send, recv, device):
    return pltpu.make_async_remote_copy(
        src_ref=src, dst_ref=dst, send_sem=send, recv_sem=recv, device_id=device, device_id_type=MESH
    )


def order_of(slot, sector_slot, orders, sectors):
    total = jnp.int32(0)
    for i in range(sectors):
        total = total + jnp.where(sector_slot[i] == slot, orders[i], 0)
    return total


def sigma_kernel(
    dims, sectors, wave_ref, base_ref, left_hbm, right_hbm, source, target, sector_slot, orders,
    out, base_all,
    wave_all, masked, left, right, product,
    send_c, got_c, send_1, got_1, mid, send_2, got_2, held, send_3, got_3,
    local, wzs, wzr, bzs, bzr, wys, wyr, bys, byr, bxs, bxr, bcs, bcr,
    cs, cr, s1, r1, s2, r2, s3, r3,
):
    nx, nc, nz, ny = dims
    me = Place(dims)
    per_owner, slab, width = out.shape
    count = left.shape[0]
    strip = ny * slab
    f32, bf16 = jnp.float32, jnp.bfloat16
    size = {"x": nx, "y": ny}
    first = (me.x * nc + me.c) * per_owner

    def rows(z, y):
        return pl.ds((z * ny + y) * slab, slab)

    def wave(z, e=0):
        return wave_all.at[:, rows(z, lax.rem(me.y + ny - e, ny)), :]

    def base(z, e=0, f=0, g=0):
        x, c, _, y = me.at(x=nx - f, c=nc - g, y=ny - e)
        return base_all.at[pl.ds((x * nc + c) * per_owner, per_owner), rows(z, y), :]

    keep_wave = pltpu.make_async_copy(wave_ref, wave(me.z), local.at[0])
    keep_base = pltpu.make_async_copy(base_ref, base(me.z), local.at[1])
    take_left = pltpu.make_async_copy(left_hbm, left, local.at[2])
    take_right = pltpu.make_async_copy(right_hbm, right, local.at[3])

    def chain(block, send, recv, up, z, src):
        shift = 1 if up else nz - 1
        return remote(
            src, block(z), send.at[0 if up else 1, z], recv.at[z], me.device(z=shift)
        )

    def wave_z(up, z, src):
        return chain(wave, wzs, wzr, up, z, src)

    def base_z(up, z, src):
        return chain(base, bzs, bzr, up, z, src)

    def wave_y(z, e, src):
        return remote(src, wave(z), wys.at[e, z], wyr.at[e, z], me.device(y=e))

    def base_y(z, e, src):
        return remote(src, base(z), bys.at[e, z], byr.at[e, z], me.device(y=e))

    def base_x(z, e, f, src):
        return remote(src, base(z, e), bxs.at[f, e, z], bxr.at[f, e, z], me.device(x=f))

    def base_c(z, e, f, g, src):
        return remote(src, base(z, e, f), bcs.at[f, e, z], bcr.at[f, e, z], me.device(c=g))

    def each_far_z(visit):
        for d in range(1, nz):

            @pl.when(me.z >= d)
            def _():
                visit(me.z - d, True)

            @pl.when(me.z + d < nz)
            def _():
                visit(me.z + d, False)

    def both_ways(start, src):
        @pl.when(me.z < nz - 1)
        def _():
            start(True, me.z, src).start()

        @pl.when(me.z > 0)
        def _():
            start(False, me.z, src).start()

    def relay(copy, block, z, up):
        copy(up, z, block(z)).wait_recv()

        @pl.when(me.z < nz - 1 if up else me.z > 0)
        def _():
            copy(up, z, block(z)).start()

    def forward_x(z, e, src):
        for f in range(1, nx):
            base_x(z, e, f, src).start()
        for g in range(1, nc):
            base_c(z, e, 0, g, src).start()

    me.greet()
    both_ways(wave_z, wave_ref)
    for e in range(1, ny):
        wave_y(me.z, e, wave_ref).start()
    keep_wave.start()
    take_left.start()
    take_right.start()
    keep_base.start()
    both_ways(base_z, base_ref)
    forward_x(me.z, 0, base_ref)

    def on_wave(z, up):
        relay(wave_z, wave, z, up)
        for e in range(1, ny):
            wave_y(z, e, wave(z)).start()

    each_far_z(on_wave)
    for e in range(1, ny):
        base_y(me.z, e, base_ref).start()

    def on_base(z, up):
        relay(base_z, base, z, up)
        forward_x(z, 0, base(z))
        for e in range(1, ny):
            base_y(z, e, base(z)).start()

    each_far_z(on_base)
    keep_wave.wait()
    take_left.wait()
    take_right.wait()
    for e in range(1, ny):

        @pl.loop(0, nz)
        def _(z):
            wave_y(z, e, wave(z, e)).wait_recv()

    row = lax.broadcasted_iota(jnp.int32, (width, width), 0)
    column = lax.broadcasted_iota(jnp.int32, (width, width), 1)
    for j in range(per_owner):
        order = order_of(first + j, sector_slot, orders, sectors)
        inside = jnp.maximum(row, column) < order
        masked[j] = jnp.where(inside, wave_all[j], jnp.zeros((), bf16))

    @pl.loop(0, count)
    def _(p):
        a = lax.rem(sector_slot[source[p]], per_owner)
        projected = jnp.dot(left[p], masked[a], preferred_element_type=f32)
        product[p] = lax.dot_general(
            projected.astype(bf16), right[p], (((1,), (1,)), ((), ())),
            preferred_element_type=f32,
        )

    landed = [sector_slot[target[p]] for p in range(count)]

    def partial_sum(slot, start, size):
        total = None
        for p in range(count):
            weight = jnp.where(landed[p] == slot, 1.0, 0.0).astype(f32)
            term = product[p, pl.ds(start, size), :] * weight
            total = term if total is None else total + term
        return total

    def axes(j):
        return ("x", "y") if j % 2 == 0 else ("y", "x")

    def zq(d):
        return lax.rem(me.z + d, nz)

    def core_copy(x, j, d):
        return remote(
            send_c.at[d, j, x], got_c.at[d, j, x], cs.at[d, j, x], cr.at[d, j, x], me.device(c=1)
        )

    def copy_1(j, d, k):
        return remote(
            send_1.at[d, j, k], got_1.at[d, j, k], s1.at[d, j, k], r1.at[d, j, k],
            me.device(**{axes(j)[0]: k}),
        )

    def copy_2(j, d, k):
        return remote(
            send_2.at[d, j, k], got_2.at[d, j, k], s2.at[d, j, k], r2.at[d, j, k],
            me.device(**{axes(j)[1]: k}),
        )

    def copy_3(j, d):
        return remote(
            send_3.at[d, j], got_3.at[d, j], s3.at[d, j], r3.at[d, j], me.device(z=d)
        )

    def unit(d):
        return lax.rem(d + 1, nz)

    if nc > 1:

        @pl.loop(0, nz)
        def _(i):
            d = unit(i)
            for j in range(per_owner):
                for x in range(nx):
                    slot = (x * nc + lax.rem(me.c + 1, nc)) * per_owner + j
                    for m in range(ny):
                        value = partial_sum(slot, pl.multiple_of(zq(d) * strip + m * slab, slab), slab)
                        send_c[d, j, x, pl.ds(m * slab, slab), :] = value.astype(bf16)
                    core_copy(x, j, d).start()

    @pl.loop(0, nz)
    def _(i):
        d = unit(i)
        for j in range(per_owner):
            n1 = size[axes(j)[0]]
            n2 = size[axes(j)[1]]
            if nc > 1:
                for x in range(nx):
                    core_copy(x, j, d).wait_recv()
            for k in list(range(1, n1)) + [0]:
                for m in range(n2):
                    if axes(j)[0] == "x":
                        x, y = lax.rem(me.x + k, nx), m
                    else:
                        x, y = m, lax.rem(me.y + k, ny)
                    offset = pl.multiple_of(y * slab, slab)
                    slot = (x * nc + me.c) * per_owner + j
                    value = partial_sum(slot, pl.multiple_of(zq(d) * strip + offset, slab), slab)
                    if nc > 1:
                        value = value + got_c[d, j, x, pl.ds(offset, slab), :].astype(f32)
                    if k:
                        send_1[d, j, k, m] = value.astype(bf16)
                    else:
                        mid[d, j, m] = value
                if k:
                    copy_1(j, d, k).start()

    for e in range(1, ny):

        @pl.loop(0, nz)
        def _(i):
            z = lax.rem(me.z + i, nz)
            base_y(z, e, base(z, e)).wait_recv()
            forward_x(z, e, base(z, e))

    @pl.loop(0, nz)
    def _(i):
        d = unit(i)
        for j in range(per_owner):
            axis_1, axis_2 = axes(j)
            n1, n2 = size[axis_1], size[axis_2]
            for k in range(1, n1):
                copy_1(j, d, k).wait_recv()
            for h in list(range(1, n2)) + [0]:
                m = lax.rem(getattr(me, axis_2) + h, n2)
                value = mid[d, j, m]
                for k in range(1, n1):
                    value = value + got_1[d, j, k, m].astype(f32)
                if h:
                    send_2[d, j, h] = value.astype(bf16)
                    copy_2(j, d, h).start()
                else:
                    held[d, j] = value

    for f in range(1, nx):
        for e in range(1):

            @pl.loop(0, nz)
            def _(z):
                base_x(z, e, f, base(z, e, f)).wait_recv()
                for g in range(1, nc):
                    base_c(z, e, f, g, base(z, e, f)).start()

    def stage_3(d, j):
        for h in range(1, size[axes(j)[1]]):
            copy_2(j, d, h).wait_recv()
        value = held[d, j]
        for h in range(1, size[axes(j)[1]]):
            value = value + got_2[d, j, h].astype(f32)
        return value

    @pl.loop(1, nz)
    def _(d):
        for j in range(per_owner):
            send_3[d, j] = stage_3(d, j).astype(bf16)
            copy_3(j, d).start()

    for f in range(1, nx):
        for e in range(1, ny):

            @pl.loop(0, nz)
            def _(i):
                z = lax.rem(me.z + i, nz)
                base_x(z, e, f, base(z, e, f)).wait_recv()
                for g in range(1, nc):
                    base_c(z, e, f, g, base(z, e, f)).start()

    row = lax.broadcasted_iota(jnp.int32, (slab, width), 0) + (me.z * ny + me.y) * slab
    column = lax.broadcasted_iota(jnp.int32, (slab, width), 1)
    for j in range(per_owner):
        value = stage_3(0, j)
        for d in range(1, nz):
            copy_3(j, d).wait_recv()
            value = value + got_3[d, j].astype(f32)
        order = order_of(first + j, sector_slot, orders, sectors)
        inside = jnp.maximum(row, column) < order
        out[j] = jnp.where(inside, value, 0.0).astype(out.dtype)

    keep_base.wait()
    for start, block in ((wave_z, wave), (base_z, base)):

        @pl.when(me.z < nz - 1)
        def _():
            @pl.loop(0, me.z + 1)
            def _(z):
                start(True, z, block(z)).wait_send()

        @pl.when(me.z > 0)
        def _():
            @pl.loop(me.z, nz)
            def _(z):
                start(False, z, block(z)).wait_send()

    @pl.loop(0, nz)
    def _(z):
        for e in range(1, ny):
            wave_y(z, e, wave(z)).wait_send()
            base_y(z, e, base(z)).wait_send()
        for e in range(ny):
            for f in range(1, nx):
                base_x(z, e, f, base(z, e)).wait_send()
            for f in range(nx):
                for g in range(1, nc):
                    base_c(z, e, f, g, base(z, e, f)).wait()

    @pl.loop(0, nz)
    def _(d):
        for j in range(per_owner):
            if nc > 1:
                for x in range(nx):
                    core_copy(x, j, d).wait_send()
            for k in range(1, size[axes(j)[0]]):
                copy_1(j, d, k).wait_send()
            for h in range(1, size[axes(j)[1]]):
                copy_2(j, d, h).wait_send()

    @pl.loop(1, nz)
    def _(d):
        for j in range(per_owner):
            copy_3(j, d).wait_send()


def sigma_and_bases(
    dims, wavefunction, sector_bases, left, right, source, target, sector_slot, orders
):
    nx, nc, nz, ny = dims
    per_owner, slab, width = wavefunction.shape
    sectors = sector_slot.shape[0]
    most = max(nx, ny)
    dma = pltpu.SemaphoreType.DMA
    bf16, f32 = jnp.bfloat16, jnp.float32
    full = (per_owner, nz * ny * slab, width)
    return pl.pallas_call(
        functools.partial(sigma_kernel, dims, sectors),
        out_shape=(
            jax.ShapeDtypeStruct((per_owner, slab, width), bf16),
            jax.ShapeDtypeStruct((sectors, nz * ny * slab, width), sector_bases.dtype),
        ),
        in_specs=[VMEM, VMEM, ANY, ANY, SMEM, SMEM, SMEM, SMEM],
        out_specs=(VMEM, ANY),
        scratch_shapes=[
            pltpu.VMEM(full, bf16),
            pltpu.VMEM(full, bf16),
            pltpu.VMEM(left.shape, bf16),
            pltpu.VMEM(right.shape, bf16),
            pltpu.VMEM(left.shape, f32),
            pltpu.VMEM((nz, per_owner, nx, ny * slab, width), bf16),
            pltpu.VMEM((nz, per_owner, nx, ny * slab, width), bf16),
            pltpu.VMEM((nz, per_owner, most, most, slab, width), bf16),
            pltpu.VMEM((nz, per_owner, most, most, slab, width), bf16),
            pltpu.VMEM((nz, per_owner, most, slab, width), f32),
            pltpu.VMEM((nz, per_owner, most, slab, width), bf16),
            pltpu.VMEM((nz, per_owner, most, slab, width), bf16),
            pltpu.VMEM((nz, per_owner, slab, width), f32),
            pltpu.VMEM((nz, per_owner, slab, width), bf16),
            pltpu.VMEM((nz, per_owner, slab, width), bf16),
        ]
        + [dma((4,))]
        + [dma((2, nz)), dma((nz,))] * 2
        + [dma((ny, nz))] * 4
        + [dma((nx, ny, nz))] * 4
        + [dma((nz, per_owner, nx))] * 2
        + [dma((nz, per_owner, most))] * 4
        + [dma((nz, per_owner))] * 2,
        compiler_params=pltpu.CompilerParams(
            collective_id=0, has_side_effects=True, vmem_limit_bytes=60 * 1024 * 1024
        ),
        name="sigma",
    )(wavefunction, sector_bases, left, right, source, target, sector_slot, orders)


def rotate_kernel(source, target, sector_slot, bases, left, rotated):
    step = pl.program_id(0)
    a = sector_slot[source[step]]
    b = sector_slot[target[step]]
    half = jnp.dot(left[0], bases[a], preferred_element_type=jnp.float32)
    rotated[0] = lax.dot_general(
        bases[b], half.astype(bases.dtype), (((0,), (0,)), ((), ())),
        preferred_element_type=jnp.float32,
    ).astype(rotated.dtype)


def rotate(bases, left, source, target, sector_slot):
    count, width, _ = left.shape
    each = pl.BlockSpec((1, width, width), lambda p, *_: (p, 0, 0))
    return pl.pallas_call(
        rotate_kernel,
        out_shape=jax.ShapeDtypeStruct(left.shape, left.dtype),
        grid_spec=pltpu.PrefetchScalarGridSpec(
            num_scalar_prefetch=3,
            grid=(count,),
            in_specs=[
                pl.BlockSpec(bases.shape, lambda p, *_: (0, 0, 0), pipeline_mode=pl.Buffered(1)),
                each,
            ],
            out_specs=each,
        ),
        compiler_params=pltpu.CompilerParams(
            dimension_semantics=("arbitrary",), vmem_limit_bytes=60 * 1024 * 1024
        ),
        name="rotate",
    )(source, target, sector_slot, bases, left)


def solution(mesh):
    dims = grid_of(mesh.shape["sector"], mesh.shape["op"])

    def per_device(
        wavefunction, sector_bases, left_env, right_env, pair_source, pair_target, sector_slot, orders
    ):
        sigma_blocks, bases = sigma_and_bases(
            dims, wavefunction, sector_bases, left_env, right_env,
            pair_source, pair_target, sector_slot, orders,
        )
        left_rotated = rotate(bases, left_env, pair_source, pair_target, sector_slot)
        return sigma_blocks, left_rotated

    placed = (
        P("sector", "op", None),
        P("sector", "op", None),
        P(("sector", "op"), None, None),
        P(("sector", "op"), None, None),
        P(("sector", "op")),
        P(("sector", "op")),
        P(),
        P(),
    )
    return jax.shard_map(
        per_device,
        mesh=mesh,
        in_specs=placed,
        out_specs=(P("sector", "op", None), P(("sector", "op"), None, None)),
        check_vma=False,
    )
```

time: 99.2 us -> 79.3 us (0.80)
  Pallas kernels: 96.3 us -> 77.7 us
    pallas_call x3 -> x2, Pallas kernels: 96.3 us -> 77.7 us  [the longest x1 67.9 us: sigma_and_bases(): pl.pallas_call(functools.partial(sigma_kernel, dims, sectors), out_shape=...]
where the time goes in v2:
time: 79.3 us; the launch traced here: 79 us
  Pallas kernels  77.7 us (98%)
    pallas_call x1, Pallas kernels, sigma_and_bases(): pl.pallas_call(functools.partial(sigma_kernel, dims, sectors), out_shape=...  67.9 us
    pallas_call x1, Pallas kernels, rotate(): pl.pallas_call(rotate_kernel, out_shape=jax.ShapeDtypeStruct(left.shape,...  9.73 us

profile of v2, /device:TPU:0, one launch (start us, length us, event | category | flops | bytes accessed | tf_op | source)
XLA Modules:
  0.0 79.0 jit_solution(13489462370221558014)
XLA Ops:
  0.6 67.9 %sigma.1 = (bf16[2,64,512]{2,1,0:T(8,128)(2,1)}, bf16[8,512,512]{2,1,0:T(8,128)(2,1)}) custom-call(bf16[2,64,512]{2,1,0:T(8,128)(2,1)} %wave_ref.1, bf16[2,64,512]{2,1,0:T(8,128)(2,1)} %base_ref.1, bf16[6,512,512]{2,1,0:T(8,128)(2,1)} %left.1, bf16[6,512,512]{2,1,0:T(8,128)(2,1)} %right_hbm.1, s32[6]{0:T(128)} %source.3, s32[6]{0:T(128)} %target.3, ...), custom_call_target="tpu_custom_call" | custom-call | tf_op jit(solution)/shard_map/sigma/pallas_call | solution.py:418
  68.6 0.0 copy-start
  68.6 9.7 %rotate.1 = bf16[6,512,512]{2,1,0:T(8,128)(2,1)} custom-call(s32[6]{0:T(128)} %source.3, s32[6]{0:T(128)} %target.3, s32[8]{0:T(128)} %sector_slot.3, bf16[8,512,512]{2,1,0:T(8,128)(2,1)} %get-tuple-element.5.bases, bf16[6,512,512]{2,1,0:T(8,128)(2,1)} %left.1), custom_call_target="tpu_custom_call" | custom-call | tf_op jit(solution)/shard_map/rotate/pallas_call | solution.py:471
  78.3 0.0 copy-done
  78.3 0.7 copy.11
Async XLA Ops:
  68.6 9.7 %copy-start = (bf16[2,64,512]{2,1,0:T(8,128)(2,1)S(1)}, bf16[2,64,512]{2,1,0:T(8,128)(2,1)}, u32[]{:S(2)}) copy-start(bf16[2,64,512]{2,1,0:T(8,128)(2,1)} %get-tuple-element.8) | copy-start | bytes 393220

commit v3 on v2

--- a/solution.py
+++ b/solution.py
@@ -70,8 +70,8 @@
 
 def sigma_kernel(
     dims, sectors, wave_ref, base_ref, left_hbm, right_hbm, source, target, sector_slot, orders,
-    out, base_all,
-    wave_all, masked, left, right, product,
+    out, base_all, half_out,
+    wave_all, masked, own_bases, half, left, right, product,
     send_c, got_c, send_1, got_1, mid, send_2, got_2, held, send_3, got_3,
     local, wzs, wzr, bzs, bzr, wys, wyr, bys, byr, bxs, bxr, bcs, bcr,
     cs, cr, s1, r1, s2, r2, s3, r3,
@@ -200,6 +200,14 @@
         inside = jnp.maximum(row, column) < order
         masked[j] = jnp.where(inside, wave_all[j], jnp.zeros((), bf16))
 
+    early = min(count // 2, nz)
+
+    def pass_on(i):
+        z = lax.rem(me.z + i, nz)
+        for e in range(1, ny):
+            base_y(z, e, base(z, e)).wait_recv()
+            forward_x(z, e, base(z, e))
+
     @pl.loop(0, count)
     def _(p):
         a = lax.rem(sector_slot[source[p]], per_owner)
@@ -208,6 +216,10 @@
             projected.astype(bf16), right[p], (((1,), (1,)), ((), ())),
             preferred_element_type=f32,
         )
+
+        @pl.when((lax.rem(p, 2) == 1) & (p < 2 * early))
+        def _():
+            pass_on(p // 2)
 
     landed = [sector_slot[target[p]] for p in range(count)]
 
@@ -290,13 +302,24 @@
                 if k:
                     copy_1(j, d, k).start()
 
-    for e in range(1, ny):
-
-        @pl.loop(0, nz)
-        def _(i):
-            z = lax.rem(me.z + i, nz)
-            base_y(z, e, base(z, e)).wait_recv()
-            forward_x(z, e, base(z, e))
+    @pl.loop(early, nz)
+    def _(i):
+        pass_on(i)
+
+    keep_base.wait()
+    take_bases = pltpu.make_async_copy(
+        base_all.at[pl.ds(first, per_owner)], own_bases, local.at[4]
+    )
+    take_bases.start()
+    take_bases.wait()
+
+    @pl.loop(0, count)
+    def _(p):
+        a = lax.rem(sector_slot[source[p]], per_owner)
+        half[p] = jnp.dot(left[p], own_bases[a], preferred_element_type=f32).astype(bf16)
+
+    give_half = pltpu.make_async_copy(half, half_out, local.at[5])
+    give_half.start()
 
     @pl.loop(0, nz)
     def _(i):
@@ -361,7 +384,7 @@
         inside = jnp.maximum(row, column) < order
         out[j] = jnp.where(inside, value, 0.0).astype(out.dtype)
 
-    keep_base.wait()
+    give_half.wait()
     for start, block in ((wave_z, wave), (base_z, base)):
 
         @pl.when(me.z < nz - 1)
@@ -420,12 +443,15 @@
         out_shape=(
             jax.ShapeDtypeStruct((per_owner, slab, width), bf16),
             jax.ShapeDtypeStruct((sectors, nz * ny * slab, width), sector_bases.dtype),
+            jax.ShapeDtypeStruct(left.shape, bf16),
         ),
         in_specs=[VMEM, VMEM, ANY, ANY, SMEM, SMEM, SMEM, SMEM],
-        out_specs=(VMEM, ANY),
+        out_specs=(VMEM, ANY, ANY),
         scratch_shapes=[
             pltpu.VMEM(full, bf16),
             pltpu.VMEM(full, bf16),
+            pltpu.VMEM(full, bf16),
+            pltpu.VMEM(left.shape, bf16),
             pltpu.VMEM(left.shape, bf16),
             pltpu.VMEM(right.shape, bf16),
             pltpu.VMEM(left.shape, f32),
@@ -440,7 +466,7 @@
             pltpu.VMEM((nz, per_owner, slab, width), bf16),
             pltpu.VMEM((nz, per_owner, slab, width), bf16),
         ]
-        + [dma((4,))]
+        + [dma((6,))]
         + [dma((2, nz)), dma((nz,))] * 2
         + [dma((ny, nz))] * 4
         + [dma((nx, ny, nz))] * 4
@@ -454,37 +480,27 @@
     )(wavefunction, sector_bases, left, right, source, target, sector_slot, orders)
 
 
-def rotate_kernel(source, target, sector_slot, bases, left, rotated):
-    step = pl.program_id(0)
-    a = sector_slot[source[step]]
-    b = sector_slot[target[step]]
-    half = jnp.dot(left[0], bases[a], preferred_element_type=jnp.float32)
+def rotate_kernel(target, sector_slot, basis, half, rotated):
     rotated[0] = lax.dot_general(
-        bases[b], half.astype(bases.dtype), (((0,), (0,)), ((), ())),
-        preferred_element_type=jnp.float32,
+        basis[0], half[0], (((0,), (0,)), ((), ())), preferred_element_type=jnp.float32
     ).astype(rotated.dtype)
 
 
-def rotate(bases, left, source, target, sector_slot):
-    count, width, _ = left.shape
+def rotate(bases, half, target, sector_slot):
+    count, width, _ = half.shape
     each = pl.BlockSpec((1, width, width), lambda p, *_: (p, 0, 0))
+    chosen = pl.BlockSpec((1, width, width), lambda p, target, slot: (slot[target[p]], 0, 0))
     return pl.pallas_call(
         rotate_kernel,
-        out_shape=jax.ShapeDtypeStruct(left.shape, left.dtype),
+        out_shape=jax.ShapeDtypeStruct(half.shape, half.dtype),
         grid_spec=pltpu.PrefetchScalarGridSpec(
-            num_scalar_prefetch=3,
-            grid=(count,),
-            in_specs=[
-                pl.BlockSpec(bases.shape, lambda p, *_: (0, 0, 0), pipeline_mode=pl.Buffered(1)),
-                each,
-            ],
-            out_specs=each,
+            num_scalar_prefetch=2, grid=(count,), in_specs=[chosen, each], out_specs=each
         ),
         compiler_params=pltpu.CompilerParams(
             dimension_semantics=("arbitrary",), vmem_limit_bytes=60 * 1024 * 1024
         ),
         name="rotate",
-    )(source, target, sector_slot, bases, left)
+    )(target, sector_slot, bases, half)
 
 
 def solution(mesh):
@@ -493,11 +509,11 @@
     def per_device(
         wavefunction, sector_bases, left_env, right_env, pair_source, pair_target, sector_slot, orders
     ):
-        sigma_blocks, bases = sigma_and_bases(
+        sigma_blocks, bases, half = sigma_and_bases(
             dims, wavefunction, sector_bases, left_env, right_env,
             pair_source, pair_target, sector_slot, orders,
         )
-        left_rotated = rotate(bases, left_env, pair_source, pair_target, sector_slot)
+        left_rotated = rotate(bases, half, pair_target, sector_slot)
         return sigma_blocks, left_rotated
 
     placed = (

time: 79.3 us -> 75.5 us (0.952)
  Pallas kernels: 77.7 us -> 73.8 us
    pallas_call x1, Pallas kernels: 9.73 us -> 7.67 us  [rotate(): pl.pallas_call(rotate_kernel, out_shape=jax.ShapeDtypeStruct(half.shape,...]
    pallas_call x1, Pallas kernels: 67.9 us -> 66.2 us  [sigma_and_bases(): pl.pallas_call(functools.partial(sigma_kernel, dims, sectors), out_shape=...]
where the time goes in v3:
time: 75.5 us; the launch traced here: 75.2 us
  Pallas kernels  73.8 us (98%)
    pallas_call x1, Pallas kernels, sigma_and_bases(): pl.pallas_call(functools.partial(sigma_kernel, dims, sectors), out_shape=...  66.2 us
    pallas_call x1, Pallas kernels, rotate(): pl.pallas_call(rotate_kernel, out_shape=jax.ShapeDtypeStruct(half.shape,...  7.67 us

profile of v3, /device:TPU:0, one launch (start us, length us, event | category | flops | bytes accessed | tf_op | source)
XLA Modules:
  0.0 75.2 jit_solution(17418951360895285023)
XLA Ops:
  0.6 66.2 %sigma.1 = (bf16[2,64,512]{2,1,0:T(8,128)(2,1)}, bf16[8,512,512]{2,1,0:T(8,128)(2,1)}, bf16[6,512,512]{2,1,0:T(8,128)(2,1)}) custom-call(bf16[2,64,512]{2,1,0:T(8,128)(2,1)} %wave_ref.1, bf16[2,64,512]{2,1,0:T(8,128)(2,1)} %base_ref.1, bf16[6,512,512]{2,1,0:T(8,128)(2,1)} %left_hbm.1, bf16[6,512,512]{2,1,0:T(8,128)(2,1)} %right_hbm.1, s32[6]{0:T(128)} %source.1, ...), custom_call_target="tpu_custom_call" | custom-call | tf_op jit(solution)/shard_map/sigma/pallas_call | solution.py:441
  66.8 0.0 copy-start
  66.8 7.7 %rotate.1 = bf16[6,512,512]{2,1,0:T(8,128)(2,1)} custom-call(s32[6]{0:T(128)} %target.3, s32[8]{0:T(128)} %sector_slot.3, bf16[8,512,512]{2,1,0:T(8,128)(2,1)} %get-tuple-element.6.basis, bf16[6,512,512]{2,1,0:T(8,128)(2,1)} %get-tuple-element.7.half), custom_call_target="tpu_custom_call" | custom-call | tf_op jit(solution)/shard_map/rotate/pallas_call | solution.py:493
  74.5 0.0 copy-done
  74.5 0.7 copy.11
Async XLA Ops:
  66.8 7.7 %copy-start = (bf16[2,64,512]{2,1,0:T(8,128)(2,1)S(1)}, bf16[2,64,512]{2,1,0:T(8,128)(2,1)}, u32[]{:S(2)}) copy-start(bf16[2,64,512]{2,1,0:T(8,128)(2,1)} %get-tuple-element.10) | copy-start | bytes 393220

commit v4 on v3

--- a/solution.py
+++ b/solution.py
@@ -73,7 +73,7 @@
     out, base_all, half_out,
     wave_all, masked, own_bases, half, left, right, product,
     send_c, got_c, send_1, got_1, mid, send_2, got_2, held, send_3, got_3,
-    local, wzs, wzr, bzs, bzr, wys, wyr, bys, byr, bxs, bxr, bcs, bcr,
+    local, hys, hyr, hzs, hzr, wzs, wzr, bzs, bzr, wys, wyr, bys, byr, bxs, bxr, bcs, bcr,
     cs, cr, s1, r1, s2, r2, s3, r3,
 ):
     nx, nc, nz, ny = dims
@@ -88,14 +88,29 @@
     def rows(z, y):
         return pl.ds((z * ny + y) * slab, slab)
 
-    def wave(z, e=0):
-        return wave_all.at[:, rows(z, lax.rem(me.y + ny - e, ny)), :]
+    low, high = pl.ds(0, per_owner // 2), pl.ds(per_owner // 2, per_owner - per_owner // 2)
+
+    def wave(z, e=0, half=low):
+        return wave_all.at[half, rows(z, lax.rem(me.y + ny - e, ny)), :]
+
+    def high_y(e):
+        return remote(
+            wave_ref.at[high], wave(me.z, 0, high), hys.at[e], hyr.at[e], me.device(y=e)
+        )
+
+    def high_block(e):
+        return lambda z: wave(z, e, high)
+
+    def high_z(e):
+        return lambda up, z, src: chain(high_block(e), hzs.at[e], hzr.at[e], up, z, src)
 
     def base(z, e=0, f=0, g=0):
         x, c, _, y = me.at(x=nx - f, c=nc - g, y=ny - e)
         return base_all.at[pl.ds((x * nc + c) * per_owner, per_owner), rows(z, y), :]
 
-    keep_wave = pltpu.make_async_copy(wave_ref, wave(me.z), local.at[0])
+    keep_wave = pltpu.make_async_copy(
+        wave_ref, wave_all.at[:, rows(me.z, me.y), :], local.at[0]
+    )
     keep_base = pltpu.make_async_copy(base_ref, base(me.z), local.at[1])
     take_left = pltpu.make_async_copy(left_hbm, left, local.at[2])
     take_right = pltpu.make_async_copy(right_hbm, right, local.at[3])
@@ -158,9 +173,12 @@
             base_c(z, e, 0, g, src).start()
 
     me.greet()
-    both_ways(wave_z, wave_ref)
     for e in range(1, ny):
-        wave_y(me.z, e, wave_ref).start()
+        high_y(e).start()
+    both_ways(wave_z, wave_ref.at[low])
+    both_ways(high_z(0), wave_ref.at[high])
+    for e in range(1, ny):
+        wave_y(me.z, e, wave_ref.at[low]).start()
     keep_wave.start()
     take_left.start()
     take_right.start()
@@ -172,7 +190,12 @@
         relay(wave_z, wave, z, up)
         for e in range(1, ny):
             wave_y(z, e, wave(z)).start()
-
+        for e in range(ny):
+            relay(high_z(e), high_block(e), z, up)
+
+    for e in range(1, ny):
+        high_y(e).wait_recv()
+        both_ways(high_z(e), wave(me.z, e, high))
     each_far_z(on_wave)
     for e in range(1, ny):
         base_y(me.z, e, base_ref).start()
@@ -385,7 +408,10 @@
         out[j] = jnp.where(inside, value, 0.0).astype(out.dtype)
 
     give_half.wait()
-    for start, block in ((wave_z, wave), (base_z, base)):
+    for e in range(1, ny):
+        high_y(e).wait_send()
+    relayed = [(wave_z, wave), (base_z, base)] + [(high_z(e), high_block(e)) for e in range(ny)]
+    for start, block in relayed:
 
         @pl.when(me.z < nz - 1)
         def _():
@@ -467,6 +493,7 @@
             pltpu.VMEM((nz, per_owner, slab, width), bf16),
         ]
         + [dma((6,))]
+        + [dma((ny,)), dma((ny,)), dma((ny, 2, nz)), dma((ny, nz))]
         + [dma((2, nz)), dma((nz,))] * 2
         + [dma((ny, nz))] * 4
         + [dma((nx, ny, nz))] * 4

time: 75.5 us -> 78 us (1.033)
  Pallas kernels: 73.8 us -> 76.3 us
    pallas_call x1, Pallas kernels: 66.2 us -> 68.6 us  [sigma_and_bases(): pl.pallas_call(functools.partial(sigma_kernel, dims, sectors), out_shape=...]
where the time goes in v4:
time: 78 us; the launch traced here: 77.6 us
  Pallas kernels  76.3 us (98%)
    pallas_call x1, Pallas kernels, sigma_and_bases(): pl.pallas_call(functools.partial(sigma_kernel, dims, sectors), out_shape=...  68.6 us
    pallas_call x1, Pallas kernels, rotate(): pl.pallas_call(rotate_kernel, out_shape=jax.ShapeDtypeStruct(half.shape,...  7.75 us

profile of v4, /device:TPU:0, one launch (start us, length us, event | category | flops | bytes accessed | tf_op | source)
XLA Modules:
  0.0 77.6 jit_solution(9028779223488493869)
XLA Ops:
  0.6 68.6 %sigma.1 = (bf16[2,64,512]{2,1,0:T(8,128)(2,1)}, bf16[8,512,512]{2,1,0:T(8,128)(2,1)}, bf16[6,512,512]{2,1,0:T(8,128)(2,1)}) custom-call(bf16[2,64,512]{2,1,0:T(8,128)(2,1)} %wave_ref.1, bf16[2,64,512]{2,1,0:T(8,128)(2,1)} %base_ref.1, bf16[6,512,512]{2,1,0:T(8,128)(2,1)} %left_hbm.1, bf16[6,512,512]{2,1,0:T(8,128)(2,1)} %right_hbm.1, s32[6]{0:T(128)} %source.1, ...), custom_call_target="tpu_custom_call" | custom-call | tf_op jit(solution)/shard_map/sigma/pallas_call | solution.py:467
  69.2 0.0 copy-start
  69.2 7.8 %rotate.1 = bf16[6,512,512]{2,1,0:T(8,128)(2,1)} custom-call(s32[6]{0:T(128)} %target.3, s32[8]{0:T(128)} %sector_slot.3, bf16[8,512,512]{2,1,0:T(8,128)(2,1)} %get-tuple-element.6.basis, bf16[6,512,512]{2,1,0:T(8,128)(2,1)} %get-tuple-element.7.half), custom_call_target="tpu_custom_call" | custom-call | tf_op jit(solution)/shard_map/rotate/pallas_call | solution.py:520
  77.0 0.0 copy-done
  77.0 0.7 copy.11
Async XLA Ops:
  69.2 7.8 %copy-start = (bf16[2,64,512]{2,1,0:T(8,128)(2,1)S(1)}, bf16[2,64,512]{2,1,0:T(8,128)(2,1)}, u32[]{:S(2)}) copy-start(bf16[2,64,512]{2,1,0:T(8,128)(2,1)} %get-tuple-element.10) | copy-start | bytes 393220
